TPU v7x, 32 devices: a whole 2x2x4 slice. The times are simulated.
32 devices in a mesh: conv: 2 (over x), seq: 8 (over z, y), head: 2 (over core).
Axes of the slice: x: 2, y: 2, z: 4, core: 2. Of those that a mesh axis runs over, the one named last changes fastest.
Arguments:
- queries: bfloat16 [3072, 2048], P(('conv', 'seq'), 'head'), parts along dimension 0, may hold values from -10 to 10, as said below
- key_states: bfloat16 [3072, 512], P(('conv', 'seq'), 'head'), parts along dimension 0, may hold values from -5 to 5, as said below
- value_states: bfloat16 [3072, 512], P(('conv', 'seq'), 'head'), parts along dimension 0, may hold values from -16 to 16
- out_weight: bfloat16 [2048, 4096], P('head'), may hold values from -0.125 to 0.125
- turn_lengths: int32 [32], P('conv'), parts along dimension 0, may hold values from 1 to 959, as said below
- block_flags: int32 [16, 8], P(('conv', 'seq')), parts along dimension 0, may hold values 0 or 1
Outputs:
- pooled: float32 [32, 4096], P(('conv', 'seq'), 'head'), parts along dimension 0
There are 2 independent parts, one for each index of `conv`. A program takes and returns all parts, laid end to end along the dimension named above; an argument that names none is the same for every part. Nothing has to cross between parts.
Inputs may be any that keep to these rules, and one draw needn't show every extreme that they name: `queries`: every entry lies within the stated bounds. `key_states`: every entry lies within the stated bounds. `turn_lengths`: the lengths sum to 1536; turn 0 has one token and turn 1, the longest, has exactly 959 tokens.
All inputs are finite; a program needn't handle non-finite values. No bound on the sum of `block_flags` on one device may be relied on, other than what follows from the above.
Results may differ from a plain program's by a relative error of at most 0.0035.
Values may be sent and summed in bfloat16 or wider, within the bound.
A program may use at most 128 MiB of HBM per device.

v0:
```python
import math
import jax
import jax.numpy as jnp
from jax import lax
from jax.sharding import PartitionSpec as P

HD = 128
big_negative = -1e30
log_two_e = 1.4426950408889634


def on_device(queries, key_states, value_states, out_weight, turn_lengths, block_flags):
    q_rows = queries.shape[0]
    heads_here = queries.shape[1] // HD
    groups = key_states.shape[1] // HD
    repeat = heads_here // groups
    factor = log_two_e / math.sqrt(HD)
    my_index = lax.axis_index("seq")
    own_pos = my_index * q_rows + jnp.arange(q_rows, dtype=jnp.int32)
    block_count = block_flags.shape[1]
    row_pick = jnp.zeros((q_rows,), jnp.int32)
    query_block = own_pos // q_rows
    grouped = queries.reshape(q_rows, groups, repeat, HD)

    def mask_for(key_start, length):
        key_pos = key_start + jnp.arange(length, dtype=jnp.int32)
        key_block = key_pos // q_rows
        hits = key_block[:, None] == jnp.arange(block_count, dtype=jnp.int32)[None, :]
        allowed = jnp.sum(jnp.where(hits[None], block_flags[:, None, :], 0), axis=2)
        allowed_rows = jnp.where(row_pick[:, None] == 1, allowed[-1][None, :], allowed[0][None, :])
        causal = key_pos[None, :] <= own_pos[:, None]
        return causal & ((key_block[None, :] == query_block[:, None]) | (allowed_rows == 1))

    def attend(state, key_rows, value_rows, key_start):
        run_top, run_sum, totals = state
        length = key_rows.shape[0]
        visible = mask_for(key_start, length)[None, None]
        logit = (
            jnp.einsum(
                "qgrd,kgd->grqk",
                grouped,
                key_rows.reshape(length, groups, HD),
                preferred_element_type=jnp.float32,
            )
            * factor
        )
        logit = jnp.where(visible, logit, big_negative)
        new_top = jnp.maximum(run_top, jnp.ceil(jnp.max(logit, axis=-1)))
        weights = jnp.where(visible, jnp.exp2(logit - new_top[..., None]), 0.0)
        rescale = jnp.exp2(run_top - new_top)
        run_sum = run_sum * rescale + jnp.sum(weights, axis=-1)
        update = jnp.einsum(
            "grqk,kgd->grqd",
            weights.astype(jnp.bfloat16),
            value_rows.reshape(length, groups, HD),
            preferred_element_type=jnp.float32,
        )
        totals = totals * rescale[..., None] + update
        return (new_top, run_sum, totals)

    start_state = (
        jnp.full((groups, repeat, q_rows), big_negative, jnp.float32),
        jnp.zeros((groups, repeat, q_rows), jnp.float32),
        jnp.zeros((groups, repeat, q_rows, HD), jnp.float32),
    )
    key_piece = lax.all_gather(key_states, "seq", axis=0, tiled=True)
    value_piece = lax.all_gather(value_states, "seq", axis=0, tiled=True)
    length = key_piece.shape[0]
    width_step = math.gcd(length, 1024)

    def one_block(number, carried):
        offset = number * width_step
        key_rows = lax.dynamic_slice_in_dim(key_piece, offset, width_step, 0)
        value_rows = lax.dynamic_slice_in_dim(value_piece, offset, width_step, 0)
        return attend(carried, key_rows, value_rows, offset)

    run_top, run_sum, totals = lax.fori_loop(0, length // width_step, one_block, start_state)
    attended_work = (
        (totals / run_sum[..., None])
        .transpose(2, 0, 1, 3)
        .reshape(q_rows, heads_here * HD)
        .astype(jnp.bfloat16)
    )
    turn_ends = jnp.cumsum(turn_lengths)
    starts = turn_ends - turn_lengths
    member = (starts[:, None] <= own_pos[None, :]) & (own_pos[None, :] < turn_ends[:, None])
    turn_share = jnp.where(member, 1.0, 0.0).astype(jnp.float32) / turn_lengths[:, None].astype(
        jnp.float32
    )
    partial_rows = jnp.dot(attended_work, out_weight, preferred_element_type=jnp.float32)
    projected_rows = lax.psum_scatter(partial_rows, "head", scatter_dimension=1, tiled=True)
    pooled_part = jnp.dot(turn_share, projected_rows, precision=lax.Precision.HIGHEST)
    return lax.psum_scatter(pooled_part, "seq", scatter_dimension=0, tiled=True)


def solution(mesh):
    in_specs = (
        P(("conv", "seq"), "head"),
        P(("conv", "seq"), "head"),
        P(("conv", "seq"), "head"),
        P("head", None),
        P("conv"),
        P(("conv", "seq"), None),
    )
    out_specs = P(("conv", "seq"), "head")
    return jax.shard_map(
        on_device, mesh=mesh, in_specs=in_specs, out_specs=out_specs, check_vma=False
    )
```

profile of v0, /device:TPU:0, one launch (start us, length us, event | category | flops | bytes accessed | tf_op | source)
XLA Modules:
  0.0 211.3 jit_solution(6904133844643909026)
XLA Ops:
  6.5 36.3 %all_gather.6 = bf16[1536,256]{1,0:T(8,128)(2,1)} all-gather(bf16[192,256]{1,0:T(8,128)(2,1)} %param.9), channel_id=1, replica_groups=mesh['conv'=2,'seq'=8,'head'=2] {'seq'}, dimensions={0}, use_global_device_ids=true | all-gather | bytes 884736 | tf_op jit(solution)/shard_map/all_gather | solution.py:66
  42.9 34.2 %all_gather.7 = bf16[1536,256]{1,0:T(8,128)(2,1)} all-gather(bf16[192,256]{1,0:T(8,128)(2,1)} %param.10), channel_id=1, replica_groups=mesh['conv'=2,'seq'=8,'head'=2] {'seq'}, dimensions={0}, use_global_device_ids=true | all-gather | bytes 884736 | tf_op jit(solution)/shard_map/all_gather | solution.py:67
  77.1 1.3 reshape.229
  78.4 0.8 copy.26
  79.2 28.0 %while.22 = (s32[]{:T(128)}, f32[2,4,192]{2,1,0:T(4,128)S(1)}, f32[2,4,192]{2,1,0:T(4,128)S(1)}, f32[2,4,192,128]{3,2,1,0:T(8,128)}, s32[1,8]{1,0:T(1,128)S(1)},...) while((s32[]{:T(128)}, f32[2,4,192]{2,1,0:T(4,128)S(1)}, ...), condition=%wide.region_5.6_spmd.clone.clone.clone, body=%wide.region_1.5_spmd.clone.clone.clone.sunk | while | flops 415462080 | bytes 14534883 | solution.py:77
  79.5 1.1 constant_dynamic-slice_fusion.4
  80.6 0.8 copy.39
  81.4 1.8 fusion.54
  83.3 1.2 fusion.55
  84.5 0.8 copy.40
  85.3 3.1 %fusion.57 = f32[2,4,192,128]{3,2,1,0:T(8,128)} fusion(bf16[512,2,128,1]{0,2,3,1:T(8,128)(2,1)} %bitcast.53, f32[2,512,192,4]{1,2,3,0:T(8,128)S(1)} %get-tuple-element.465, f32[2,4,192]{2,1,0:T(4,128)S(1)} %ceil_maximum_fusion.2, pred[192,512]{1,0:T(8,128)(4,1)S(1)} %or_and_fusion.2, f32[2,4,192,128]{3,2,1,0:T(8,128)} %get-tuple-element.485, ...), kind=kOutput, calls=%fused_computation.9.clone.1 | convolution fusion | flops 206635008 | bytes 5091329 | tf_op jit(solution)/shard_map/while/body/eval_jaxpr/grqk,kgd->grqd/dot_general | solution.py:52
  88.8 1.1 constant_dynamic-slice_fusion.4
  89.8 0.8 copy.39
  90.7 1.8 fusion.54
  92.5 1.2 fusion.55
  93.8 0.8 copy.40
  94.6 3.2 %fusion.57 = f32[2,4,192,128]{3,2,1,0:T(8,128)} fusion(bf16[512,2,128,1]{0,2,3,1:T(8,128)(2,1)} %bitcast.53, f32[2,512,192,4]{1,2,3,0:T(8,128)S(1)} %get-tuple-element.465, f32[2,4,192]{2,1,0:T(4,128)S(1)} %ceil_maximum_fusion.2, pred[192,512]{1,0:T(8,128)(4,1)S(1)} %or_and_fusion.2, f32[2,4,192,128]{3,2,1,0:T(8,128)} %get-tuple-element.485, ...), kind=kOutput, calls=%fused_computation.9.clone.1 | convolution fusion | flops 206635008 | bytes 5091329 | tf_op jit(solution)/shard_map/while/body/eval_jaxpr/grqk,kgd->grqd/dot_general | solution.py:52
  98.1 1.1 constant_dynamic-slice_fusion.4
  99.2 0.8 copy.39
  100.1 1.8 fusion.54
  101.9 1.2 fusion.55
  103.1 0.8 copy.40
  104.0 3.2 %fusion.57 = f32[2,4,192,128]{3,2,1,0:T(8,128)} fusion(bf16[512,2,128,1]{0,2,3,1:T(8,128)(2,1)} %bitcast.53, f32[2,512,192,4]{1,2,3,0:T(8,128)S(1)} %get-tuple-element.465, f32[2,4,192]{2,1,0:T(4,128)S(1)} %ceil_maximum_fusion.2, pred[192,512]{1,0:T(8,128)(4,1)S(1)} %or_and_fusion.2, f32[2,4,192,128]{3,2,1,0:T(8,128)} %get-tuple-element.485, ...), kind=kOutput, calls=%fused_computation.9.clone.1 | convolution fusion | flops 206635008 | bytes 5091329 | tf_op jit(solution)/shard_map/while/body/eval_jaxpr/grqk,kgd->grqd/dot_general | solution.py:52
  107.2 1.4 fusion.19
  108.6 0.3 copy.28
  109.2 6.9 %fusion.35 = f32[192,4096]{1,0:T(8,128)} fusion(bf16[192,1024]{1,0:T(8,128)(2,1)S(1)} %convert_element_type.26, bf16[1024,4096]{1,0:T(8,128)(2,1)} %param.11), kind=kOutput, calls=%fused_computation.51 | convolution fusion | flops 1610612736 | bytes 11927552 | tf_op jit(solution)/shard_map/dot_general | solution.py:90
  116.1 0.6 copy-done.1
  117.0 11.5 %reduce-scatter.2.cloned.1.call-done = f32[192,2048]{1,0:T(8,128)} async-done(((f32[192,4096]{1,0:T(8,128)}), f32[192,2048]{1,0:T(8,128)}) %reduce-scatter.2.cloned.1.call-update) | async-done | bytes 1572880 | tf_op jit(solution)/shard_map/reduce_scatter | solution.py:91
  128.5 2.9 %fusion.20 = f32[16,2048]{1,0:T(8,128)} fusion(f32[192,2048]{1,0:T(8,128)} %reduce-scatter.2.cloned.1.call-done, f32[16]{0:T(128)S(1)} %get-tuple-element.393, s32[192]{0:T(256)S(1)} %iota_add_fusion.2, s32[16]{0:T(128)S(1)} %reduce.6, s32[16]{0:T(128)S(1)} %get-tuple-element.392), kind=kOutput, calls=%fused_computation.34 | convolution fusion | flops 75512832 | bytes 1704896 | tf_op jit(solution)/shard_map/dot_general | solution.py:92
  131.4 0.6 dynamic-slice
  132.6 70.4 %all-reduce.3.cloned.1.call-done = f32[16,2048]{1,0:T(8,128)} async-done(((f32[16,2048]{1,0:T(8,128)}), f32[16,2048]{1,0:T(8,128)}) %all-reduce.3.cloned.1.call-update) | async-done | bytes 131088
  203.0 1.5 constant_dynamic-slice_fusion.2
  (42 shorter events, 1.6 us)
Async XLA Ops:
  6.5 72.6 %copy-start = (s32[1,8]{1,0:T(1,128)S(1)}, s32[1,8]{1,0:T(1,128)}, u32[]{:S(2)}) copy-start(s32[1,8]{1,0:T(1,128)} %param.13) | copy-start | bytes 100
  6.5 121.9 %reduce-scatter.2.cloned.1.call-start = ((), (), s32[]{:S(2)}) async-start(), calls=%async_computation.1 | async-start | bytes 4718592 | tf_op jit(solution)/shard_map/reduce_scatter | solution.py:91
  116.1 0.7 copy-start.1
  116.1 15.3 %copy-start.2 = (u32[32]{0:T(128)S(1)}, u32[32]{0:T(128)}, u32[]{:S(2)}) copy-start(u32[32]{0:T(128)} %constant.141) | copy-start | bytes 388
  116.1 86.9 %all-reduce.3.cloned.1.call-start = ((), (), s32[]{:S(2)}) async-start(), calls=%async_computation.2 | async-start | bytes 262144
Sparse Core Ops, SparseCore 0:
  116.2 12.2 reduce-scatter.1
  132.2 70.7 all-reduce.2
where the time goes:
time: 212 us; the launch traced here: 211 us
  waiting for transfers between devices  81.9 us (39%)
  blocking collectives  70.6 us (33%)
  matrix products  24.8 us (12%)
  between operations  14.1 us (7%)
  local copies, waits for them, and re-layouts  13.6 us (6%)
  other arithmetic  6.13 us (3%)
    unnamed x3, waiting for transfers between devices  70.4 us
    all_gather x1, blocking collectives, on_device(): key_piece = lax.all_gather(key_states, 'seq', axis=0, tiled=True)  36.3 us
    all_gather x1, blocking collectives, on_device(): value_piece = lax.all_gather(value_states, 'seq', axis=0, tiled=True)  34.2 us
    reduce_scatter x1, waiting for transfers between devices, on_device(): lax.psum_scatter(partial_rows, 'head', scatter_dimension=1, tiled=True)  11.5 us
    dot_general x3, matrix products, attend(): jnp.einsum('grqk,kgd->grqd', weights.astype(jnp.bfloat16), value_rows.res...  9.53 us
    dot_general x1, matrix products, on_device(): jnp.dot(attended_work, out_weight, preferred_element_type=jnp.float32)  6.85 us
    dynamic_slice x6, local copies, waits for them, and re-layouts, one_block(): value_rows = lax.dynamic_slice_in_dim(value_piece, offset, width_step, 0)  5.76 us
    dot_general x3, matrix products, attend(): jnp.einsum('qgrd,kgd->grqk', grouped, key_rows.reshape(length, groups, HD...  5.5 us
  transfers between devices with their start and end apart: 2, of which 2 were waited for; matrix products, arithmetic and copies ran while one was open for 0% of the time, Pallas kernels for 0%

commit v1 on v0

--- a/solution.py
+++ b/solution.py
@@ -63,7 +63,14 @@
         jnp.zeros((groups, repeat, q_rows), jnp.float32),
         jnp.zeros((groups, repeat, q_rows, HD), jnp.float32),
     )
-    key_piece = lax.all_gather(key_states, "seq", axis=0, tiled=True)
+    ways, here = (lax.axis_size("seq"), lax.axis_index("seq"))
+    key_piece, reach = (key_states, 1)
+    while reach < ways:
+        theirs = lax.ppermute(key_piece, "seq", [(d, d ^ reach) for d in range(ways)])
+        mine_first = jnp.concatenate([key_piece, theirs], axis=0)
+        theirs_first = jnp.concatenate([theirs, key_piece], axis=0)
+        key_piece = jnp.where(here & reach == 0, mine_first, theirs_first)
+        reach = 2 * reach
     value_piece = lax.all_gather(value_states, "seq", axis=0, tiled=True)
     length = key_piece.shape[0]
     width_step = math.gcd(length, 1024)

time: 212 us -> 195 us (0.920)
  blocking collectives: 70.6 us -> 40.4 us
  starting transfers between devices: 0.04 us -> 7.49 us
  waiting for transfers between devices: 81.9 us -> 85.5 us
    all_gather x1 -> x0, blocking collectives: 36.3 us -> none  [on_device(): key_piece = lax.all_gather(key_states, 'seq', axis=0, tiled=True)]
    ppermute x0 -> x3, waiting for transfers between devices: none -> 7.79 us  [on_device(): lax.ppermute(key_piece, 'seq', [(d, d ^ reach) for d in range(ways)])]
    ppermute x0 -> x3, starting transfers between devices: none -> 7.45 us  [on_device(): lax.ppermute(key_piece, 'seq', [(d, d ^ reach) for d in range(ways)])]
    all_gather x1, blocking collectives: 34.2 us -> 40.4 us  [on_device(): value_piece = lax.all_gather(value_states, 'seq', axis=0, tiled=True)]
    reduce_scatter x1, waiting for transfers between devices: 11.5 us -> 7.25 us  [on_device(): lax.psum_scatter(partial_rows, 'head', scatter_dimension=1, tiled=True)]
    unnamed x9 -> x10, local copies, waits for them, and re-layouts: 3.42 us -> 4.42 us
  transfers between devices with their start and end apart: 2 -> 5, of which waited for: 2 -> 4; matrix products, arithmetic and copies ran while one was open for 0% -> 1% of each run, Pallas kernels for 0% -> 0%
where the time goes in v1:
time: 195 us; the launch traced here: 194 us
  waiting for transfers between devices  85.5 us (44%)
  blocking collectives  40.4 us (21%)
  matrix products  24.6 us (13%)
  local copies, waits for them, and re-layouts  14.7 us (8%)
  between operations  14.1 us (7%)
  starting transfers between devices  7.49 us (4%)
  other arithmetic  7.44 us (4%)
    unnamed x3, waiting for transfers between devices  70.4 us
    all_gather x1, blocking collectives, on_device(): value_piece = lax.all_gather(value_states, 'seq', axis=0, tiled=True)  40.4 us
    dot_general x3, matrix products, attend(): jnp.einsum('grqk,kgd->grqd', weights.astype(jnp.bfloat16), value_rows.res...  9.53 us
    ppermute x3, waiting for transfers between devices, on_device(): lax.ppermute(key_piece, 'seq', [(d, d ^ reach) for d in range(ways)])  7.79 us
    ppermute x3, starting transfers between devices, on_device(): lax.ppermute(key_piece, 'seq', [(d, d ^ reach) for d in range(ways)])  7.45 us
    reduce_scatter x1, waiting for transfers between devices, on_device(): lax.psum_scatter(partial_rows, 'head', scatter_dimension=1, tiled=True)  7.25 us
    dot_general x1, matrix products, on_device(): jnp.dot(attended_work, out_weight, preferred_element_type=jnp.float32)  6.85 us
    dynamic_slice x6, local copies, waits for them, and re-layouts, one_block(): value_rows = lax.dynamic_slice_in_dim(value_piece, offset, width_step, 0)  5.46 us
  transfers between devices with their start and end apart: 5, of which 4 were waited for; matrix products, arithmetic and copies ran while one was open for 1% of the time, Pallas kernels for 0%

profile of v1, /device:TPU:0, one launch (start us, length us, event | category | flops | bytes accessed | tf_op | source)
XLA Modules:
  0.0 194.4 jit_solution(6553951902228426111)
XLA Ops:
  6.5 1.0 copy.30
  7.5 3.0 %collective-permute-start = (bf16[192,256]{0,1:T(8,128)(2,1)S(1)}, bf16[192,256]{0,1:T(8,128)(2,1)S(1)}, u32[]{:S(2)}, u32[]{:S(2)}) collective-permute-start(bf16[192,256]{0,1:T(8,128)(2,1)S(1)} %copy.30), channel_id=1, source_target_pairs={{0,2},{2,0},{4,6},{6,4},{8,10},{10,8},{12,14},{14,12},{1,3},{3,1},... | collective-permute-start | bytes 294920 | tf_op jit(solution)/shard_map/ppermute | solution.py:69
  10.6 3.5 %collective-permute-done = bf16[192,256]{0,1:T(8,128)(2,1)S(1)} collective-permute-done((bf16[192,256]{0,1:T(8,128)(2,1)S(1)}, bf16[192,256]{0,1:T(8,128)(2,1)S(1)}, u32[]{:S(2)}, u32[]{:S(2)}) %collective-permute-start) | collective-permute-done | bytes 98336 | tf_op jit(solution)/shard_map/ppermute | solution.py:69
  14.2 1.9 collective-permute-start.1
  16.1 4.3 %collective-permute-done.1 = bf16[384,256]{0,1:T(8,128)(2,1)S(1)} collective-permute-done((bf16[384,256]{0,1:T(8,128)(2,1)S(1)}, bf16[384,256]{0,1:T(8,128)(2,1)S(1)}, u32[]{:S(2)}, u32[]{:S(2)}) %collective-permute-start.1) | collective-permute-done | bytes 196640 | tf_op jit(solution)/shard_map/ppermute | solution.py:69
  20.5 2.6 %collective-permute-start.2 = (bf16[768,256]{0,1:T(8,128)(2,1)S(1)}, bf16[768,256]{0,1:T(8,128)(2,1)S(1)}, u32[]{:S(2)}, u32[]{:S(2)}) collective-permute-start(bf16[768,256]{0,1:T(8,128)(2,1)S(1)} %maximum_select_fusion.1), channel_id=1, source_target_pairs={{0,8},{2,10},{4,12},{6,14},{8,0},{10,2},{12,4},{14,6},{1,9},{3,11}... | collective-permute-start | bytes 1179656 | tf_op jit(solution)/shard_map/ppermute | solution.py:69
  23.1 1.3 reshape.229
  25.1 40.4 %all_gather.3 = bf16[1536,256]{1,0:T(8,128)(2,1)} all-gather(bf16[192,256]{1,0:T(8,128)(2,1)} %param.10), channel_id=1, replica_groups=mesh['conv'=2,'seq'=8,'head'=2] {'seq'}, dimensions={0}, use_global_device_ids=true | all-gather | bytes 884736 | tf_op jit(solution)/shard_map/all_gather | solution.py:74
  65.5 1.1 maximum_select_fusion
  66.6 27.9 %while.22 = (s32[]{:T(128)}, f32[2,4,192]{2,1,0:T(4,128)S(1)}, f32[2,4,192]{2,1,0:T(4,128)S(1)}, f32[2,4,192,128]{3,2,1,0:T(8,128)}, s32[1,8]{1,0:T(1,128)S(1)},...) while((s32[]{:T(128)}, f32[2,4,192]{2,1,0:T(4,128)S(1)}, ...), condition=%wide.region_5.6_spmd.clone.clone.clone, body=%wide.region_1.5_spmd.clone.clone.clone.sunk | while | flops 415462080 | bytes 14010599 | solution.py:84
  66.9 1.0 constant_dynamic-slice_fusion.5
  67.9 1.8 fusion.54
  69.7 1.2 fusion.55
  70.9 1.0 constant_dynamic-slice_fusion.6
  71.9 0.8 copy.43
  72.7 3.1 %fusion.57 = f32[2,4,192,128]{3,2,1,0:T(8,128)} fusion(bf16[512,2,128,1]{0,2,3,1:T(8,128)(2,1)} %bitcast.53, f32[2,512,192,4]{1,2,3,0:T(8,128)S(1)} %get-tuple-element.460, f32[2,4,192]{2,1,0:T(4,128)S(1)} %ceil_maximum_fusion.2, pred[192,512]{1,0:T(8,128)(4,1)S(1)} %or_and_fusion.2, f32[2,4,192,128]{3,2,1,0:T(8,128)} %get-tuple-element.479, ...), kind=kOutput, calls=%fused_computation.9.clone.1 | convolution fusion | flops 206635008 | bytes 5091329 | tf_op jit(solution)/shard_map/while/body/eval_jaxpr/grqk,kgd->grqd/dot_general | solution.py:52
  76.1 1.0 constant_dynamic-slice_fusion.5
  77.1 1.8 fusion.54
  78.9 1.2 fusion.55
  80.1 1.0 constant_dynamic-slice_fusion.6
  82.0 3.2 %fusion.57 = f32[2,4,192,128]{3,2,1,0:T(8,128)} fusion(bf16[512,2,128,1]{0,2,3,1:T(8,128)(2,1)} %bitcast.53, f32[2,512,192,4]{1,2,3,0:T(8,128)S(1)} %get-tuple-element.460, f32[2,4,192]{2,1,0:T(4,128)S(1)} %ceil_maximum_fusion.2, pred[192,512]{1,0:T(8,128)(4,1)S(1)} %or_and_fusion.2, f32[2,4,192,128]{3,2,1,0:T(8,128)} %get-tuple-element.479, ...), kind=kOutput, calls=%fused_computation.9.clone.1 | convolution fusion | flops 206635008 | bytes 5091329 | tf_op jit(solution)/shard_map/while/body/eval_jaxpr/grqk,kgd->grqd/dot_general | solution.py:52
  85.5 1.0 constant_dynamic-slice_fusion.5
  86.5 1.8 fusion.54
  88.2 1.2 fusion.55
  89.5 1.0 constant_dynamic-slice_fusion.6
  91.3 3.2 %fusion.57 = f32[2,4,192,128]{3,2,1,0:T(8,128)} fusion(bf16[512,2,128,1]{0,2,3,1:T(8,128)(2,1)} %bitcast.53, f32[2,512,192,4]{1,2,3,0:T(8,128)S(1)} %get-tuple-element.460, f32[2,4,192]{2,1,0:T(4,128)S(1)} %ceil_maximum_fusion.2, pred[192,512]{1,0:T(8,128)(4,1)S(1)} %or_and_fusion.2, f32[2,4,192,128]{3,2,1,0:T(8,128)} %get-tuple-element.479, ...), kind=kOutput, calls=%fused_computation.9.clone.1 | convolution fusion | flops 206635008 | bytes 5091329 | tf_op jit(solution)/shard_map/while/body/eval_jaxpr/grqk,kgd->grqd/dot_general | solution.py:52
  94.5 1.4 fusion.19
  96.5 6.9 %fusion.35 = f32[192,4096]{1,0:T(8,128)} fusion(bf16[192,1024]{1,0:T(8,128)(2,1)S(1)} %convert_element_type.26, bf16[1024,4096]{1,0:T(8,128)(2,1)} %param.11), kind=kOutput, calls=%fused_computation.54 | convolution fusion | flops 1610612736 | bytes 11927552 | tf_op jit(solution)/shard_map/dot_general | solution.py:97
  104.3 7.3 %reduce-scatter.2.cloned.1.call-done = f32[192,2048]{1,0:T(8,128)} async-done(((f32[192,4096]{1,0:T(8,128)}), f32[192,2048]{1,0:T(8,128)}) %reduce-scatter.2.cloned.1.call-update) | async-done | bytes 1572880 | tf_op jit(solution)/shard_map/reduce_scatter | solution.py:98
  111.5 2.9 %fusion.20 = f32[16,2048]{1,0:T(8,128)} fusion(f32[192,2048]{1,0:T(8,128)} %reduce-scatter.2.cloned.1.call-done, f32[16]{0:T(128)S(1)} %get-tuple-element.391, s32[192]{0:T(256)S(1)} %iota_add_fusion.2, s32[16]{0:T(128)S(1)} %reduce.6, s32[16]{0:T(128)S(1)} %get-tuple-element.390), kind=kOutput, calls=%fused_computation.37 | convolution fusion | flops 75512832 | bytes 1704896 | tf_op jit(solution)/shard_map/dot_general | solution.py:99
  115.7 70.4 %all-reduce.3.cloned.1.call-done = f32[16,2048]{1,0:T(8,128)} async-done(((f32[16,2048]{1,0:T(8,128)}), f32[16,2048]{1,0:T(8,128)}) %all-reduce.3.cloned.1.call-update) | async-done | bytes 131088
  186.1 1.5 constant_dynamic-slice_fusion.2
  (51 shorter events, 5.8 us)
Async XLA Ops:
  6.5 60.1 %copy-start = (s32[1,8]{1,0:T(1,128)S(1)}, s32[1,8]{1,0:T(1,128)}, u32[]{:S(2)}) copy-start(s32[1,8]{1,0:T(1,128)} %param.13) | copy-start | bytes 100
  6.5 105.0 %reduce-scatter.2.cloned.1.call-start = ((), (), s32[]{:S(2)}) async-start(), calls=%async_computation.1 | async-start | bytes 4718592 | tf_op jit(solution)/shard_map/reduce_scatter | solution.py:98
  7.5 6.5 %collective-permute-start = (bf16[192,256]{0,1:T(8,128)(2,1)S(1)}, bf16[192,256]{0,1:T(8,128)(2,1)S(1)}, u32[]{:S(2)}, u32[]{:S(2)}) collective-permute-start(bf16[192,256]{0,1:T(8,128)(2,1)S(1)} %copy.30), channel_id=1, source_target_pairs={{0,2},{2,0},{4,6},{6,4},{8,10},{10,8},{12,14},{14,12},{1,3},{3,1},... | collective-permute-start | bytes 294920 | tf_op jit(solution)/shard_map/ppermute | solution.py:69
  14.2 6.2 %collective-permute-start.1 = (bf16[384,256]{0,1:T(8,128)(2,1)S(1)}, bf16[384,256]{0,1:T(8,128)(2,1)S(1)}, u32[]{:S(2)}, u32[]{:S(2)}) collective-permute-start(bf16[384,256]{0,1:T(8,128)(2,1)S(1)} %maximum_select_fusion.2), channel_id=1, source_target_pairs={{0,4},{2,6},{4,0},{6,2},{8,12},{10,14},{12,8},{14,10},{1,5},{3,7},... | collective-permute-start | bytes 589832 | tf_op jit(solution)/shard_map/ppermute | solution.py:69
  20.5 45.1 %collective-permute-start.2 = (bf16[768,256]{0,1:T(8,128)(2,1)S(1)}, bf16[768,256]{0,1:T(8,128)(2,1)S(1)}, u32[]{:S(2)}, u32[]{:S(2)}) collective-permute-start(bf16[768,256]{0,1:T(8,128)(2,1)S(1)} %maximum_select_fusion.1), channel_id=1, source_target_pairs={{0,8},{2,10},{4,12},{6,14},{8,0},{10,2},{12,4},{14,6},{1,9},{3,11}... | collective-permute-start | bytes 1179656 | tf_op jit(solution)/shard_map/ppermute | solution.py:69
  103.4 0.7 copy-start.1
  103.4 11.1 %copy-start.2 = (u32[32]{0:T(128)S(1)}, u32[32]{0:T(128)}, u32[]{:S(2)}) copy-start(u32[32]{0:T(128)} %constant.146) | copy-start | bytes 388
  103.4 82.7 %all-reduce.3.cloned.1.call-start = ((), (), s32[]{:S(2)}) async-start(), calls=%async_computation.2 | async-start | bytes 262144
Sparse Core Ops, SparseCore 0:
  103.5 7.9 reduce-scatter.1
  115.2 70.8 all-reduce.2
